TPU v7x, 256 devices: a whole 4x4x8 slice. The times are simulated.
256 devices in a mesh: sector: 64 (over x_lo, y, z), radial: 2 (over x_hi), col: 2 (over core).
Axes of the slice: x: 4 (x_hi: 2, x_lo: 2; x = x_hi * 2 + x_lo), y: 4, z: 8, core: 2. Of those that a mesh axis runs over, the one named last changes fastest.
Arguments:
- correction_guess: float32 [8, 3, 256, 32, 128], P('col', None, 'sector', 'radial'), may hold values from -24 to 24
- ritz_residual: float32 [8, 3, 256, 32, 128], P('col', None, 'sector', 'radial'), may hold values from -36 to 36
- ritz_basis: float32 [8, 3, 256, 32, 128], P('col', None, 'sector', 'radial'), may hold values from -8 to 8
- diagonal: float32 [256, 32, 128], P('sector', 'radial'), may hold values from 0.25 to 2
- coupling: float32 [3, 3], replicated, may hold values from -0.3 to 2, as said below
- class_ids: int32 [64], P('sector'), may hold values from 0 to 7
- class_stiffness: float32 [8], replicated, may hold values from 0.7 to 1.4
- shifts: float32 [8], P('col'), may hold values from 0.1 to 0.5
- contact_dest: int32 [32768, 1], P(('sector', 'radial')), may hold values from 0 to 63; in each aligned block of 256 rows (0 to 255, 256 to 511, ...) at most 8 rows name the same one
- contact_source: int32 [32768], P(('sector', 'radial')), may hold values from 0 to 8191
- contact_target: int32 [32768], P(('sector', 'radial')), may hold values from 0 to 8191
- contact_stiffness: float32 [32768], P(('sector', 'radial')), may hold values from 0.5 to 2
Outputs:
- correction: float32 [8, 3, 256, 32, 128], P('col', None, 'sector', 'radial')
- inner_residual: float32 [8, 3, 256, 32, 128], P('col', None, 'sector', 'radial')
Inputs may be any that keep to these rules, and one draw needn't show every extreme that they name: `contact_dest`: in the rows of one device no sector is named more than 8 times, and one sector exactly 8 times. `coupling`: diagonal entries between 1 and 2.
All inputs are finite; a program needn't handle non-finite values.
Results may differ from a plain program's by a relative error of at most 0.0002.
Values sent between devices are 32-bit elements; how exact they have to be, the bound alone decides.
A program may use at most 64 MiB of HBM per device.

v0:
```python
import functools

import jax
import jax.numpy as jnp
from jax import lax
from jax.experimental import pallas as pl
from jax.experimental.pallas import tpu as pltpu
from jax.sharding import Mesh
from jax.sharding import PartitionSpec as P

SECTOR = ("sector_0", "sector_1", "sector_2")
SECTOR_RADIAL = ("sector_0", "sector_1", "sector_2", "radial")
DAMPING = 0.7
NX, NY, NZ = 2, 4, 8
NP = NX * NY
F32 = jnp.float32
BF16 = jnp.bfloat16
MESH_ID = pl.DeviceIdType.MESH
NT = (((1,), (1,)), ((), ()))


def split2(x):
    hi = x.astype(BF16)
    return hi, (x - hi.astype(F32)).astype(BF16)


def iota(shape, dim):
    return lax.broadcasted_iota(jnp.int32, shape, dim).astype(F32)


def kernel(
    dofs,
    dst_r, src_r, tgt_r, kst_r, kap, cid, cst, shf, c0_h, rho_h, q_h, dg_h,
    oc_h, or_h,
    u, rho, q, dg, ij, w, d,
    ut, qt, dgt, dgs, ijt, dt,
    us, qs, ijs, ds,
    ur, qr, ijr, dr, rsnd,
    lsm, rsm, ltm, rtm, wbuf,
    cs1a, cr1a, cs2a, cr2a, cs1, cr1, cs2, cr2,
    rm, rs1, rr1, rs2, rr2,
    cf, st_s, mt_s, acf,
    ld_sem, out_sem, snd, rcv,
):
    x = lax.axis_index("sector_0")
    y = lax.axis_index("sector_1")
    z = lax.axis_index("sector_2")
    ri = lax.axis_index("radial")
    me_col = lax.axis_index("col")
    p = x * NY + y
    pq = ri * NP + p

    def zpeer(k):
        return {"sector_2": (z + k) % NZ}

    def plane(k):
        o = (pq + k) % (2 * NP)
        return {"radial": o // NP, "sector_0": (o // NY) % NX, "sector_1": o % NY}

    def ppeer(k):
        o = (p + k) % NP
        return {"sector_0": o // NY, "sector_1": o % NY}

    c1 = (z + 1) // NZ
    c2 = (y + c1) // NY
    nxt = {"sector_2": (z + 1) % NZ, "sector_1": (y + c1) % NY, "sector_0": (x + c2) % NX}
    b1 = 1 - (z + NZ - 1) // NZ
    b2 = 1 - (y + NY - b1) // NY
    prv = {"sector_2": (z + NZ - 1) % NZ, "sector_1": (y + NY - b1) % NY, "sector_0": (x + NX - b2) % NX}
    across = {"radial": 1 - ri}
    twin = {"col": 1 - me_col}

    barrier = pltpu.get_barrier_semaphore()

    def sig(dev):
        pl.semaphore_signal(barrier, inc=1, device_id=dev, device_id_type=MESH_ID)

    for k in range(1, NZ):
        sig(zpeer(k))
    for k in range(1, 2 * NP):
        sig(plane(k))
    sig(nxt)
    sig(prv)
    sig(twin)

    loads = [
        pltpu.make_async_copy(q_h, q.at[pl.ds(0, 4)], ld_sem.at[0]),
        pltpu.make_async_copy(c0_h, u, ld_sem.at[1]),
        pltpu.make_async_copy(dg_h, dg, ld_sem.at[2]),
        pltpu.make_async_copy(rho_h, rho, ld_sem.at[3]),
    ]
    for c in loads:
        c.start()

    count = [0]
    pending = []

    def rcopy(src, dst, dev, idx):
        return pltpu.make_async_remote_copy(
            src_ref=src, dst_ref=dst, send_sem=snd.at[idx], recv_sem=rcv.at[idx],
            device_id=dev, device_id_type=MESH_ID,
        )

    def send(src, dst, dev):
        idx = count[0]
        count[0] += 1
        c = rcopy(src, dst, dev, idx)
        c.start()
        pending.append(c)
        return c

    def group(n, peer, src_of, dst):
        idx = count[0]
        count[0] += 1

        def one(k, carry):
            rcopy(src_of(k), dst, peer(k), idx).start()
            return carry

        lax.fori_loop(1, n, one, 0)
        return idx

    def await_group(buf, n, idx):
        part = buf.at[pl.ds(0, n)]
        pltpu.make_async_copy(part, part, rcv.at[idx]).wait()

    def drain_group(buf, n, idx):
        part = buf.at[pl.ds(0, n)]
        pltpu.make_async_copy(part, part, snd.at[idx]).wait()

    stiff = cst[cid[0]]

    meta = [r[...].astype(F32) for r in (dst_r, src_r, tgt_r, kst_r)]

    def flat_row(m):
        return jnp.concatenate([m[0:1, :], m[1:2, :]], axis=1)

    dest = flat_row(meta[0])
    later = iota((128, 256), 1)
    rank = jnp.zeros((1, 256), F32)
    for h in range(2):
        column = jnp.broadcast_to(meta[0][h : h + 1, :], (128, 128)).T
        column = jnp.concatenate([column, column], axis=1)
        hit = (column == dest) & (iota((128, 256), 0) + 128.0 * h < later)
        rank = rank + jnp.sum(jnp.where(hit, 1.0, 0.0), axis=0, keepdims=True)
    dp = jnp.floor(dest * 0.125)
    slot = rank * 64.0 + (dest - 8.0 * dp) * 8.0 + dp
    source, target, kst = flat_row(meta[1]), flat_row(meta[2]), flat_row(meta[3])
    s_row = jnp.floor(source * (1.0 / 128.0))
    t_row = jnp.floor(target * (1.0 / 128.0))
    k_hi = kst.astype(BF16).astype(F32)
    k_mid = (kst - k_hi).astype(BF16).astype(F32)
    k_lo = kst - k_hi - k_mid
    rows = jnp.concatenate(
        [s_row, source - 128.0 * s_row, t_row, target - 128.0 * t_row, k_hi, k_mid, k_lo, jnp.ones((1, 256), F32)],
        axis=0,
    ).astype(BF16)
    onehot = jnp.where(iota((512, 256), 0) == slot, 1.0, 0.0).astype(BF16)
    packed = lax.dot_general(rows, onehot, NT, preferred_element_type=F32)
    valid = packed[7:8, :] > 0.5
    src_row = jnp.where(valid, packed[0:1, :], -1.0)
    picks = jnp.where(iota((128, 512), 0) == packed[1:2, :], 1.0, 0.0).astype(BF16)
    lsm[...] = jnp.concatenate([picks, picks], axis=0)
    rsm[...] = jnp.where(iota((64, 512), 0) == src_row, 1.0, 0.0)
    tgt = packed[2:3, :] * 128.0 + packed[3:4, :]
    kpk = packed[4:5, :] + packed[5:6, :] + packed[6:7, :]

    pl.semaphore_wait(barrier, (NZ - 1) + (2 * NP - 1) + 3)

    def edge_rows(ref, j, c):
        top = ref[j, c, pl.ds(15, 4, stride=16), :]
        bottom = ref[j, c, pl.ds(0, 4, stride=16), :]
        return jnp.where(ri == 0, top, bottom)

    def pack_radial(ref, out, spare):
        for j in range(4):
            tail = spare if (spare is not None and j == 0) else jnp.zeros((4, 128), F32)
            out[j] = jnp.concatenate([edge_rows(ref, j, c) for c in range(3)] + [tail], axis=0)

    def send_tangent(ref, dst):
        a = send(ref.at[:, :, pl.ds(48, 16), :], dst.at[0], nxt)
        b = send(ref.at[:, :, pl.ds(0, 16), :], dst.at[1], prv)
        return a, b

    def gather(ref, base):
        def column(j, carry):
            xs = jnp.concatenate([ref[j, c] for c in range(3)], axis=0)
            both = jnp.concatenate(split2(xs), axis=1)
            got = jnp.dot(both, lsm[...], preferred_element_type=F32)
            for c in range(3):
                picked = jnp.sum(got[c * 64 : (c + 1) * 64] * rsm[...], axis=0, keepdims=True)
                for sh in range(4):
                    wbuf[base + j * 4 + c, pl.ds(sh, 1), :] = picked[:, sh * 128 : (sh + 1) * 128]
            return carry

        for j in range(4):
            column(j, 0)

    def spare_rows(base, j, row):
        for sh in range(4):
            wbuf[base + j * 4 + 3, pl.ds(sh, 1), :] = row[:, sh * 128 : (sh + 1) * 128]

    def message(base):
        m = wbuf[pl.ds(base, 16)].reshape(64, 128)
        turned = jnp.concatenate([m, m], axis=0).T
        lane = lax.broadcasted_iota(jnp.int32, (64, 128), 1)
        return jnp.where(lane < 64, turned[0:64], turned[64:128])

    def unpack(m):
        both = jnp.concatenate([m, pltpu.roll(m, 64, 1)], axis=0).T
        return both[0:64].reshape(4, 16, 128)

    def fold_dots(ref, vref):
        def block(b, acc):
            c, r = b // 8, pl.multiple_of((b % 8) * 8, 8)
            qv = [q[i, c, pl.ds(r, 8), :] for i in range(8)]
            out = []
            for j in range(4):
                v = vref[j, c, pl.ds(r, 8), :]
                for i in range(8):
                    out.append(acc[j * 8 + i] + qv[i] * v)
            return tuple(out)

        acc = lax.fori_loop(0, 24, block, tuple(jnp.zeros((8, 128), F32) for _ in range(32)))
        for k in range(32):
            ref[pl.ds(k, 1), :] = jnp.sum(acc[k], axis=0, keepdims=True)

    def gram(ref, scale):
        pairs = [(a, b) for a in range(8) for b in range(a, 8)]

        def block(b, acc):
            c, r = b // 8, pl.multiple_of((b % 8) * 8, 8)
            qv = [q[i, c, pl.ds(r, 8), :] for i in range(8)]
            sv = qv if scale is None else [t * ij[scale, c, pl.ds(r, 8), :] for t in qv]
            return tuple(acc[n] + sv[a] * qv[e] for n, (a, e) in enumerate(pairs))

        acc = lax.fori_loop(0, 24, block, tuple(jnp.zeros((8, 128), F32) for _ in pairs))
        for n, (a, e) in enumerate(pairs):
            row = jnp.sum(acc[n], axis=0, keepdims=True)
            ref[pl.ds(a * 8 + e, 1), :] = row
            if a != e:
                ref[pl.ds(e * 8 + a, 1), :] = row

    def lane_totals(block):
        return jnp.sum(block.T, axis=0, keepdims=True)

    def spread(row):
        return jnp.broadcast_to(row * (1.0 / dofs), (128, 128)).T

    def reduce_start(rnd, nr):
        idx = group(
            NZ, zpeer, lambda k: rs1.at[rnd, pl.ds(0, nr)], rr1.at[rnd, z, pl.ds(0, nr)]
        )
        rr1[rnd, z, pl.ds(0, nr)] = rs1[rnd, pl.ds(0, nr)]
        return idx

    def reduce_middle(rnd, nr, idx):
        part = rr1.at[rnd, pl.ds(0, NZ - 1), pl.ds(0, nr)]
        pltpu.make_async_copy(part, part, rcv.at[idx]).wait()
        total = rr1[rnd, 0, pl.ds(0, nr)]
        for k in range(1, NZ):
            total = total + rr1[rnd, k, pl.ds(0, nr)]
        rs2[rnd, pl.ds(0, nr)] = total
        idx2 = group(
            2 * NP, plane, lambda k: rs2.at[rnd, pl.ds(0, nr)], rr2.at[rnd, pq, pl.ds(0, nr)]
        )
        rr2[rnd, pq, pl.ds(0, nr)] = total
        return idx2

    def reduce_end(rnd, nr, idx):
        part = rr2.at[rnd, pl.ds(0, 2 * NP - 1), pl.ds(0, nr)]
        pltpu.make_async_copy(part, part, rcv.at[idx]).wait()
        total = rr2[rnd, 0, pl.ds(0, nr)]
        for k in range(1, 2 * NP):
            total = total + rr2[rnd, k, pl.ds(0, nr)]
        return total

    def reduce_drain(rnd, nr, idx1, idx2):
        part = rr1.at[rnd, pl.ds(0, NZ - 1), pl.ds(0, nr)]
        pltpu.make_async_copy(part, part, snd.at[idx1]).wait()
        part = rr2.at[rnd, pl.ds(0, 2 * NP - 1), pl.ds(0, nr)]
        pltpu.make_async_copy(part, part, snd.at[idx2]).wait()

    def exchange_start(s1, r1):
        idx = group(NZ, zpeer, lambda k: s1.at[(z + k) % NZ], r1.at[z])
        r1[z] = s1[z]
        return idx

    def exchange_middle(r1, s2, r2, idx, g):
        await_group(r1, NZ - 1, idx)
        for k in range(NP):
            for e in range(g):
                s2[k, pl.ds(e * 8, 8), :] = r1[:, e * 8 + k, :]
        idx2 = group(NP, ppeer, lambda k: s2.at[(p + k) % NP], r2.at[p])
        r2[p] = s2[p]
        return idx2

    loads[0].wait()
    swap_q = send(q.at[pl.ds(0, 4)], q.at[pl.ds(4, 4)], twin)
    halo_q = send_tangent(q.at[pl.ds(0, 4)], qt.at[:, pl.ds(0, 4)])
    loads[1].wait()
    halo_c = send_tangent(u, ut)
    loads[2].wait()
    splat = jnp.full((8, 128), stiff, F32)
    dgs[0] = jnp.concatenate([dg[48:64, :], splat], axis=0)
    dgs[1] = jnp.concatenate([dg[0:16, :], splat], axis=0)
    halo_d = (send(dgs.at[0], dgt.at[0], nxt), send(dgs.at[1], dgt.at[1], prv))
    dg_edge = jnp.where(ri == 0, dg[pl.ds(15, 4, stride=16), :], dg[pl.ds(0, 4, stride=16), :])
    pack_radial(u, rsnd.at[0], dg_edge)
    pack_radial(q, rsnd.at[1], None)
    side_c = send(rsnd.at[0], ur, across)
    side_q = send(rsnd.at[1], qr.at[pl.ds(0, 4)], across)

    gather(u, 0)
    gather(q, 16)
    got = jnp.dot(jnp.concatenate(split2(dg[...]), axis=1), lsm[...], preferred_element_type=F32)
    spare_rows(0, 0, jnp.sum(got * rsm[...], axis=0, keepdims=True))
    spare_rows(0, 1, tgt)
    spare_rows(0, 2, jnp.full((1, 512), stiff, F32))
    spare_rows(0, 3, kpk)
    for j in range(4):
        spare_rows(16, j, jnp.zeros((1, 512), F32))
    for e in range(2):
        cs1a[:, pl.ds(e * 8, 8), :] = message(16 * e).reshape(NZ, 8, 128)
    xa1 = exchange_start(cs1a, cr1a)

    for j in range(4):
        for c in range(3):
            ij[j, c] = 1.0 / (stiff * 6.0 * kap[c, c] + dg[...] - shf[j])

    swap_q.wait_recv()
    rm[pl.ds(96, 32), :] = jnp.zeros((32, 128), F32)
    fold_dots(rm, u)
    gram(rm.at[pl.ds(32, 64)], None)
    rs1[0, 0] = lane_totals(rm[pl.ds(0, 128), :])
    ra1 = reduce_start(0, 1)

    for j in range(4):
        gram(rm.at[pl.ds(128 + j * 64, 64)], j)

    ra2 = reduce_middle(0, 1, ra1)
    xa2 = exchange_middle(cr1a, cs2a, cr2a, xa1, 2)

    for e in range(2):
        rs1[1, 1 + e] = lane_totals(rm[pl.ds(128 + e * 128, 128), :])

    for c in halo_d + halo_q + halo_c + (side_c, side_q):
        c.wait_recv()
    swap_t = send(qt.at[:, pl.ds(0, 4)], qt.at[:, pl.ds(4, 4)], twin)
    swap_r = send(qr.at[pl.ds(0, 4)], qr.at[pl.ds(4, 4)], twin)
    for side in range(2):
        sv = jnp.concatenate([dgt[side, 16:24, :], dgt[side, 16:24, :]], axis=0)
        dv = dgt[side, 0:16, :]
        for j in range(4):
            for c in range(3):
                ijt[side, j, c] = 1.0 / (sv * 6.0 * kap[c, c] + dv - shf[j])
    dv = ur[0, 12:16, :]
    base = jnp.concatenate([stiff * 6.0 * kap[c, c] + dv for c in range(3)] + [jnp.full((4, 128), 2.0, F32)], axis=0)
    for j in range(4):
        ijr[j] = 1.0 / (base - shf[j])

    await_group(cr2a, NP - 1, xa2)
    us[...] = unpack(cr2a[:, pl.ds(0, 8), :].reshape(64, 128))
    qs[pl.ds(0, 4)] = unpack(cr2a[:, pl.ds(8, 8), :].reshape(64, 128))
    swap_s = send(qs.at[pl.ds(0, 4)], qs.at[pl.ds(4, 4)], twin)
    dv = us[0, 12:16, :]
    sv = us[2, 12:16, :]
    base = jnp.concatenate([sv * 6.0 * kap[c, c] + dv for c in range(3)] + [jnp.full((4, 128), 2.0, F32)], axis=0)
    for j in range(4):
        ijs[j] = 1.0 / (base - shf[j])
    kr = us[3, 12:16, :]
    for sh in range(4):
        tv = us[1, 12 + sh : 13 + sh, :]
        tr = jnp.floor(tv * (1.0 / 128.0))
        tl = tv - 128.0 * tr
        lanes = slice(sh * 128, (sh + 1) * 128)
        rtm[:, lanes] = jnp.where(iota((64, 128), 0) == tr, 1.0, 0.0) * kr[sh : sh + 1, :]
        lands = jnp.where(iota((128, 128), 0) == tl, 1.0, 0.0).astype(BF16)
        ltm[:, lanes] = lands
        ltm[:, 512 + sh * 128 : 640 + sh * 128] = lands

    total = reduce_end(0, 1, ra2)
    wide = spread(total[0])
    acf[...] = wide[0:32].reshape(4, 8, 128)
    st_s[...] = wide[32:96].reshape(8, 8, 128)

    def mix(coef, j, qv):
        n = qv[0].shape[0]
        acc = None
        for i in range(8):
            term = jnp.broadcast_to(coef[j, pl.ds(i, 1), :], (n, 128)) * qv[i]
            acc = term if acc is None else acc + term
        return acc

    regions = (
        (12, lambda b: (b // 4, pl.multiple_of((b % 4) * 16, 16)),
         lambda r, j, a: r[j, a[0], pl.ds(a[1], 16), :], (u, q, ij, d)),
        (6, lambda b: (b // 3, b % 3),
         lambda r, j, a: r[a[0], j, a[1]], (ut, qt, ijt, dt)),
        (1, lambda b: b, lambda r, j, a: r[j], (us, qs, ijs, ds)),
        (1, lambda b: b, lambda r, j, a: r[j], (ur, qr, ijr, dr)),
    )

    def put(region, j, a, v):
        if region == 0:
            u[j, a[0], pl.ds(a[1], 16), :] = v
        elif region == 1:
            ut[a[0], j, a[1]] = v
        elif region == 2:
            us[j] = v
        else:
            ur[j] = v

    def first_update(which):
        for n in which:
            blocks, place, get, (ru, rq, _, _) = regions[n]

            def step(b, carry):
                a = place(b)
                qv = [get(rq, i, a) for i in range(8)]
                for j in range(4):
                    put(n, j, a, get(ru, j, a) - mix(acf, j, qv))
                return carry

            lax.fori_loop(0, blocks, step, 0)

    def update(rnd):
        for n in range(4):
            blocks, place, get, (ru, rq, rj, rd) = regions[n]

            def step(b, carry):
                a = place(b)
                qv = [get(rq, i, a) for i in range(8)]
                for j in range(4):
                    new = get(ru, j, a) + DAMPING * get(rd.at[rnd], j, a)
                    new = new + get(rj, j, a) * mix(cf.at[0], j, qv) - mix(cf.at[1], j, qv)
                    put(n, j, a, new)
                return carry

            lax.fori_loop(0, blocks, step, 0)

    for c in halo_c:
        c.wait_send()
        pending[:] = [t for t in pending if t is not c]
    first_update((0,))
    swap_t.wait_recv()
    swap_r.wait_recv()
    swap_s.wait_recv()
    first_update((1, 2, 3))

    row_in = lax.broadcasted_iota(jnp.int32, (64, 128), 0) % 16
    lane_in = lax.broadcasted_iota(jnp.int32, (64, 128), 1)
    edge = row_in == 15 * (1 - ri)

    def apply(dref):
        def column(j, carry):
            hs = []
            for c in range(3):
                hrow, lrow = [], []
                for sh in range(4):
                    v = us[j, pl.ds(c * 4 + sh, 1), :]
                    a = rtm[:, sh * 128 : (sh + 1) * 128] * v
                    ah, al = split2(a)
                    hrow.append(ah)
                    lrow.append(al)
                hs.append(jnp.concatenate(hrow + lrow, axis=1))
            touch = lax.dot_general(jnp.concatenate(hs, axis=0), ltm[...], NT, preferred_element_type=F32)
            xs = [u[j, c] for c in range(3)]
            for c in range(3):
                v = xs[c]
                before = jnp.concatenate([ut[0, j, c], v[0:48]], axis=0)
                after = jnp.concatenate([v[16:64], ut[1, j, c]], axis=0)
                lap = 6.0 * v - before - after
                lap = lap - jnp.where(row_in == 0, 0.0, pltpu.roll(v, 1, 0))
                lap = lap - jnp.where(row_in == 15, 0.0, pltpu.roll(v, 63, 0))
                beside = jnp.concatenate(
                    [jnp.broadcast_to(ur[j, pl.ds(c * 4 + t, 1), :], (16, 128)) for t in range(4)], axis=0
                )
                lap = lap - jnp.where(edge, beside, 0.0)
                lap = lap - jnp.where(lane_in == 0, 0.0, pltpu.roll(v, 1, 1))
                lap = lap - jnp.where(lane_in == 127, 0.0, pltpu.roll(v, 127, 1))
                mixed = kap[c, c] * lap
                for e in range(3):
                    if e != c:
                        mixed = mixed + kap[c, e] * xs[e]
                out = stiff * mixed + (dg[...] - shf[j]) * v + touch[c * 64 : (c + 1) * 64]
                w[j, c] = out
                dref[j, c] = -(rho[j, c] + out) * ij[j, c]
            return carry

        lax.fori_loop(0, 4, column, 0)

    def coefficients(row, final):
        wide = spread(row)
        for j in range(4):
            b = wide[j * 8 : j * 8 + 8]
            e = wide[32 + j * 8 : 40 + j * 8]
            for i in range(8):
                e = e + mt_s[j, i] * b[i : i + 1, :]
            a = acf[j]
            if final:
                cf[0, j] = b
                cf[1, j] = a - DAMPING * e
            else:
                se = st_s[0] * e[0:1, :]
                for i in range(1, 8):
                    se = se + st_s[i] * e[i : i + 1, :]
                cf[0, j] = DAMPING * b
                cf[1, j] = DAMPING * (2.0 * e - se)
                acf[j] = a + DAMPING * (e - se)

    loads[3].wait()
    drains = []
    for rnd in range(3):
        last = rnd == 2
        nr = 3 if rnd == 0 else 1
        dref = d.at[rnd]
        apply(dref)
        if not last:
            pack_radial(dref, rsnd.at[2 + rnd], None)
            halo = send_tangent(dref, dt.at[rnd])
            side = send(rsnd.at[2 + rnd], dr.at[rnd], across)
            gather(dref, 0)
            cs1[rnd] = message(0).reshape(NZ, 8, 128)
            x1 = exchange_start(cs1.at[rnd], cr1.at[rnd])
        fold_dots(rm, w)
        fold_dots(rm.at[pl.ds(32, 32)], dref)
        rs1[rnd + 1, 0] = lane_totals(rm[pl.ds(0, 128), :])
        r1 = reduce_start(rnd + 1, nr)
        if not last:
            x2 = None
        r2 = reduce_middle(rnd + 1, nr, r1)
        drains.append((rnd + 1, nr, r1, r2))
        if not last:
            x2 = exchange_middle(cr1.at[rnd], cs2.at[rnd], cr2.at[rnd], x1, 1)
            for c in halo + (side,):
                c.wait_recv()
        total = reduce_end(rnd + 1, nr, r2)
        if rnd == 0:
            for e in range(2):
                mt_s[pl.ds(2 * e, 2)] = spread(total[1 + e]).reshape(2, 8, 8, 128)
        coefficients(total[0], last)
        if not last:
            await_group(cr2.at[rnd], NP - 1, x2)
            ds[rnd] = unpack(cr2[rnd].reshape(64, 128))
            update(rnd)
            drains.append((rnd, x1, x2))

    def finish(b, carry):
        c, r = b // 4, pl.multiple_of((b % 4) * 16, 16)
        here = (c, pl.ds(r, 16))
        qv = [q[i, c, pl.ds(r, 16), :] for i in range(8)]
        for j in range(4):
            res = mix(cf.at[0], j, qv) - rho[j, c, pl.ds(r, 16), :] - w[j, c, pl.ds(r, 16), :]
            new = u[j, c, pl.ds(r, 16), :] + DAMPING * res * ij[j, c, pl.ds(r, 16), :] + mix(cf.at[1], j, qv)
            w[j, c, pl.ds(r, 16), :] = res
            rho[j, c, pl.ds(r, 16), :] = new
        return carry

    lax.fori_loop(0, 12, finish, 0)
    outs = [
        pltpu.make_async_copy(rho, oc_h, out_sem.at[0]),
        pltpu.make_async_copy(w, or_h, out_sem.at[1]),
    ]
    for c in outs:
        c.start()
    for c in pending:
        c.wait_send()
    drain_group(cr1a, NZ - 1, xa1)
    drain_group(cr2a, NP - 1, xa2)
    reduce_drain(0, 1, ra1, ra2)
    for t in drains:
        if len(t) == 4:
            reduce_drain(*t)
        else:
            drain_group(cr1.at[t[0]], NZ - 1, t[1])
            drain_group(cr2.at[t[0]], NP - 1, t[2])
    for c in outs:
        c.wait()


def body(
    correction_guess, ritz_residual, ritz_basis, diagonal, coupling, class_ids,
    class_stiffness, shifts, contact_dest, contact_source, contact_target, contact_stiffness,
):
    cols, chans, tang, rloc, ax = correction_guess.shape
    devices = NX * NY * NZ * 2
    dofs = float(chans * tang * rloc * ax * devices)
    flat = (cols, chans, tang * rloc, ax)
    vm = pltpu.VMEM
    own = (4, 3, 64, 128)
    sheet = (4, 3, 16, 128)
    small = (4, 16, 128)
    scratch = [
        vm(own, F32), vm(own, F32), vm((8, 3, 64, 128), F32), vm((64, 128), F32), vm(own, F32), vm(own, F32),
        vm((3,) + own, F32),
        vm((2,) + sheet, F32), vm((2, 8, 3, 16, 128), F32), vm((2, 24, 128), F32), vm((2, 24, 128), F32),
        vm((2,) + sheet, F32), vm((2, 2) + sheet, F32),
        vm(small, F32), vm((8, 16, 128), F32), vm(small, F32), vm((2,) + small, F32),
        vm(small, F32), vm((8, 16, 128), F32), vm(small, F32), vm((2,) + small, F32), vm((4,) + small, F32),
        vm((256, 512), BF16), vm((64, 512), F32), vm((128, 1024), BF16), vm((64, 512), F32), vm((32, 4, 128), F32),
        vm((NZ, 16, 128), F32), vm((NZ, 16, 128), F32), vm((NP, 16, 128), F32), vm((NP, 16, 128), F32),
        vm((2, NZ, 8, 128), F32), vm((2, NZ, 8, 128), F32), vm((2, NP, 8, 128), F32), vm((2, NP, 8, 128), F32),
        vm((384, 128), F32), vm((4, 3, 1, 128), F32), vm((4, NZ, 3, 1, 128), F32), vm((4, 3, 1, 128), F32),
        vm((4, 2 * NP, 3, 1, 128), F32),
        vm((2, 4, 8, 128), F32), vm((8, 8, 128), F32), vm((4, 8, 8, 128), F32), vm((4, 8, 128), F32),
        pltpu.SemaphoreType.DMA((4,)), pltpu.SemaphoreType.DMA((2,)),
        pltpu.SemaphoreType.DMA((36,)), pltpu.SemaphoreType.DMA((36,)),
    ]
    anyspace = pl.BlockSpec(memory_space=pl.ANY)
    smem = pl.BlockSpec(memory_space=pltpu.SMEM)
    correction, residual = pl.pallas_call(
        functools.partial(kernel, dofs),
        out_shape=(jax.ShapeDtypeStruct(flat, F32), jax.ShapeDtypeStruct(flat, F32)),
        in_specs=[pl.BlockSpec(memory_space=pltpu.VMEM)] * 4 + [smem] * 4 + [pl.BlockSpec(memory_space=pltpu.HBM)] * 4,
        out_specs=(anyspace, anyspace),
        scratch_shapes=scratch,
        compiler_params=pltpu.CompilerParams(collective_id=0, has_side_effects=True, vmem_limit_bytes=16 * 1024 * 1024),
        name="sweeps",
    )(
        contact_dest.reshape(2, 128), contact_source.reshape(2, 128), contact_target.reshape(2, 128),
        contact_stiffness.reshape(2, 128), coupling, class_ids, class_stiffness, shifts,
        *(pltpu.with_memory_space_constraint(a, pltpu.HBM) for a in (
            correction_guess.reshape(flat), ritz_residual.reshape(flat), ritz_basis.reshape(flat),
            diagonal.reshape(tang * rloc, ax),
        )),
    )
    shape = correction_guess.shape
    return correction.reshape(shape), residual.reshape(shape)


def solution(mesh):
    split = Mesh(
        mesh.devices.reshape(NX, NY, NZ, mesh.shape["radial"], mesh.shape["col"]),
        ("sector_0", "sector_1", "sector_2", "radial", "col"),
    )
    field = P("col", None, SECTOR, "radial", None)
    placed = (
        field, field, field, P(SECTOR, "radial", None), P(), P(SECTOR), P(), P("col"),
        P(SECTOR_RADIAL, None), P(SECTOR_RADIAL), P(SECTOR_RADIAL), P(SECTOR_RADIAL),
    )
    return jax.shard_map(body, mesh=split, in_specs=placed, out_specs=(field, field), check_vma=False)
```

profile of v0, /device:TPU:2, one launch (start us, length us, event | category | flops | bytes accessed | tf_op | source)
XLA Modules:
  0.0 70.6 jit_solution(3805401457728071331)
XLA Ops:
  1.3 0.0 copy-start.4
  1.3 0.0 copy-start.6
  1.3 0.0 copy-start.2
  1.3 0.0 copy-start.3
  1.3 0.0 copy-start
  1.3 0.0 copy-start.1
  1.3 0.0 copy-start.5
  1.3 0.6 copy-done.4
  2.0 0.0 copy-done.6
  2.0 0.0 copy-done.2
  2.0 0.0 copy-done.3
  2.0 0.0 copy-done
  2.0 0.0 copy-done.1
  2.0 0.0 copy-done.5
  2.0 67.1 %sweeps.1 = (f32[4,3,64,128]{3,2,1,0:T(8,128)S(1)}, f32[4,3,64,128]{3,2,1,0:T(8,128)S(1)}) custom-call(s32[2,128]{1,0:T(2,128)S(1)} %bitcast.12, s32[2,128]{1,0:T(2,128)S(1)} %bitcast.13, s32[2,128]{1,0:T(2,128)S(1)} %bitcast.14, f32[2,128]{1,0:T(2,128)S(1)} %bitcast.15, f32[3,3]{1,0:T(4,128)S(1)} %copy-done, s32[1]{0:T(128)S(6)} %copy.16.cid, ...), custom_call_target="tpu_custom_call" | custom-call | tf_op jit(solution)/shard_map/sweeps/pallas_call | solution.py:612
  69.1 0.7 %copy.17 = f32[4,3,4,16,128]{4,3,2,1,0:T(8,128)} copy(f32[4,3,4,16,128]{4,3,2,1,0:T(8,128)S(1)} %bitcast.11) | data formatting | bytes 786432
  69.9 0.7 %copy.18 = f32[4,3,4,16,128]{4,3,2,1,0:T(8,128)} copy(f32[4,3,4,16,128]{4,3,2,1,0:T(8,128)S(1)} %bitcast.10) | data formatting | bytes 786432
Async XLA Ops:
  1.3 0.7 copy-start.4
  1.3 0.7 copy-start.6
  1.3 0.7 copy-start.2
  1.3 0.7 copy-start.3
  1.3 0.7 copy-start
  1.3 0.7 %copy-start.1 = (s32[256,1]{0,1:T(1,128)S(1)}, s32[256,1]{0,1:T(1,128)}, u32[]{:S(2)}) copy-start(s32[256,1]{0,1:T(1,128)} %param.20) | copy-start | bytes 3076
  1.3 0.7 copy-start.5
where the time goes:
time: 70.8 us; the launch traced here: 70.6 us
  Pallas kernels  67.1 us (95%)
  local copies, waits for them, and re-layouts  2.2 us (3%)
  between operations  1.35 us (2%)
    pallas_call x1, Pallas kernels, body(): pl.pallas_call(functools.partial(kernel, dofs), out_shape=(jax.ShapeDtype...  67.1 us
    unnamed x16, local copies, waits for them, and re-layouts  2.2 us

commit v1 on v0

--- a/solution.py
+++ b/solution.py
@@ -12,7 +12,25 @@
 SECTOR_RADIAL = ("sector_0", "sector_1", "sector_2", "radial")
 DAMPING = 0.7
 NX, NY, NZ = 2, 4, 8
-NP = NX * NY
+NS = NX * NY * NZ
+SIZES = {"sector_0": NX, "sector_1": NY, "sector_2": NZ, "radial": 2}
+
+
+def peer_offsets():
+    along_x = {(0, 0): 0, (1, 0): 1, (0, 1): 2, (1, 1): 1}
+    found = []
+    for dr in range(2):
+        for dx in range(NX):
+            for dy in range(NY):
+                for dz in range(NZ):
+                    hops = along_x[dx, dr] + min(dy, NY - dy) + min(dz, NZ - dz)
+                    steps = (("sector_0", dx), ("sector_1", dy), ("sector_2", dz), ("radial", dr))
+                    if hops:
+                        found.append((-hops, tuple(t for t in steps if t[1])))
+    return [t[1] for t in sorted(found, key=lambda t: t[0])]
+
+
+OFFSETS = peer_offsets()
 F32 = jnp.float32
 BF16 = jnp.bfloat16
 MESH_ID = pl.DeviceIdType.MESH
@@ -36,9 +54,9 @@
     ut, qt, dgt, dgs, ijt, dt,
     us, qs, ijs, ds,
     ur, qr, ijr, dr, rsnd,
-    lsm, rsm, ltm, rtm, wbuf,
-    cs1a, cr1a, cs2a, cr2a, cs1, cr1, cs2, cr2,
-    rm, rs1, rr1, rs2, rr2,
+    lsm, rsm, ltm, rtm, wbuf, amat, land, krow,
+    pa, ra, pb, rb, pc, rc, pd, rd,
+    rm,
     cf, st_s, mt_s, acf,
     ld_sem, out_sem, snd, rcv,
 ):
@@ -47,19 +65,21 @@
     z = lax.axis_index("sector_2")
     ri = lax.axis_index("radial")
     me_col = lax.axis_index("col")
-    p = x * NY + y
-    pq = ri * NP + p
-
-    def zpeer(k):
-        return {"sector_2": (z + k) % NZ}
-
-    def plane(k):
-        o = (pq + k) % (2 * NP)
-        return {"radial": o // NP, "sector_0": (o // NY) % NX, "sector_1": o % NY}
-
-    def ppeer(k):
-        o = (p + k) % NP
-        return {"sector_0": o // NY, "sector_1": o % NY}
+
+    here = {"sector_0": x, "sector_1": y, "sector_2": z, "radial": ri}
+
+    def peer(offset):
+        place = {}
+        for name, step in offset:
+            at = here[name] + step
+            place[name] = jnp.where(at >= SIZES[name], at - SIZES[name], at)
+        return place
+
+    def sector_of(place):
+        return (place.get("sector_0", x) * NY + place.get("sector_1", y)) * NZ + place.get("sector_2", z)
+
+    me = sector_of({})
+    me_row = ri * NS + me
 
     c1 = (z + 1) // NZ
     c2 = (y + c1) // NY
@@ -75,12 +95,8 @@
     def sig(dev):
         pl.semaphore_signal(barrier, inc=1, device_id=dev, device_id_type=MESH_ID)
 
-    for k in range(1, NZ):
-        sig(zpeer(k))
-    for k in range(1, 2 * NP):
-        sig(plane(k))
-    sig(nxt)
-    sig(prv)
+    for offset in OFFSETS:
+        sig(peer(offset))
     sig(twin)
 
     loads = [
@@ -109,24 +125,37 @@
         pending.append(c)
         return c
 
-    def group(n, peer, src_of, dst):
+    def exchange(planes, rbuf, same, other):
+        (a0, an), (b0, bn) = same, other
         idx = count[0]
-        count[0] += 1
-
-        def one(k, carry):
-            rcopy(src_of(k), dst, peer(k), idx).start()
-            return carry
-
-        lax.fori_loop(1, n, one, 0)
-        return idx
-
-    def await_group(buf, n, idx):
-        part = buf.at[pl.ds(0, n)]
-        pltpu.make_async_copy(part, part, rcv.at[idx]).wait()
-
-    def drain_group(buf, n, idx):
-        part = buf.at[pl.ds(0, n)]
-        pltpu.make_async_copy(part, part, snd.at[idx]).wait()
+        count[0] += 2
+        for offset in OFFSETS:
+            place = peer(offset)
+            across_slab = "radial" in place
+            first, num = (b0, bn) if across_slab else (a0, an)
+            if num == 0:
+                continue
+            row = sector_of(place)
+            rcopy(
+                planes.at[pl.ds(first, num), pl.ds(row, 1)],
+                rbuf.at[pl.ds(first, num), pl.ds(me_row, 1)],
+                place, idx + int(across_slab),
+            ).start()
+        for e in range(a0, a0 + an):
+            rbuf[e, pl.ds(me_row, 1), :] = planes[e, pl.ds(me, 1), :]
+
+        def finish(sem):
+            if an:
+                part = rbuf.at[pl.ds(a0, an), pl.ds(0, NS - 1)]
+                pltpu.make_async_copy(part, part, sem.at[idx]).wait()
+            if bn:
+                part = rbuf.at[pl.ds(b0, bn), pl.ds(0, NS)]
+                pltpu.make_async_copy(part, part, sem.at[idx + 1]).wait()
+
+        drains.append(lambda: finish(snd))
+        return lambda: finish(rcv)
+
+    drains = []
 
     stiff = cst[cid[0]]
 
@@ -143,8 +172,7 @@
         column = jnp.concatenate([column, column], axis=1)
         hit = (column == dest) & (iota((128, 256), 0) + 128.0 * h < later)
         rank = rank + jnp.sum(jnp.where(hit, 1.0, 0.0), axis=0, keepdims=True)
-    dp = jnp.floor(dest * 0.125)
-    slot = rank * 64.0 + (dest - 8.0 * dp) * 8.0 + dp
+    slot = rank * 64.0 + dest
     source, target, kst = flat_row(meta[1]), flat_row(meta[2]), flat_row(meta[3])
     s_row = jnp.floor(source * (1.0 / 128.0))
     t_row = jnp.floor(target * (1.0 / 128.0))
@@ -165,8 +193,6 @@
     tgt = packed[2:3, :] * 128.0 + packed[3:4, :]
     kpk = packed[4:5, :] + packed[5:6, :] + packed[6:7, :]
 
-    pl.semaphore_wait(barrier, (NZ - 1) + (2 * NP - 1) + 3)
-
     def edge_rows(ref, j, c):
         top = ref[j, c, pl.ds(15, 4, stride=16), :]
         bottom = ref[j, c, pl.ds(0, 4, stride=16), :]
@@ -210,109 +236,75 @@
         both = jnp.concatenate([m, pltpu.roll(m, 64, 1)], axis=0).T
         return both[0:64].reshape(4, 16, 128)
 
-    def fold_dots(ref, vref):
+    def fold_dots(ref, vref, half):
+        lead = half * 4
+
         def block(b, acc):
-            c, r = b // 8, pl.multiple_of((b % 8) * 8, 8)
-            qv = [q[i, c, pl.ds(r, 8), :] for i in range(8)]
-            out = []
-            for j in range(4):
-                v = vref[j, c, pl.ds(r, 8), :]
-                for i in range(8):
-                    out.append(acc[j * 8 + i] + qv[i] * v)
+            c, r = b // 4, pl.multiple_of((b % 4) * 16, 16)
+            out = list(acc)
+            for e in range(2):
+                qv = [q[lead + i, c, pl.ds(r + 8 * e, 8), :] for i in range(4)]
+                vv = [vref[j, c, pl.ds(r + 8 * e, 8), :] for j in range(4)]
+                for j in range(4):
+                    for i in range(4):
+                        out[j * 4 + i] = out[j * 4 + i] + qv[i] * vv[j]
             return tuple(out)
 
-        acc = lax.fori_loop(0, 24, block, tuple(jnp.zeros((8, 128), F32) for _ in range(32)))
-        for k in range(32):
-            ref[pl.ds(k, 1), :] = jnp.sum(acc[k], axis=0, keepdims=True)
-
-    def gram(ref, scale):
-        pairs = [(a, b) for a in range(8) for b in range(a, 8)]
+        acc = lax.fori_loop(0, 12, block, tuple(jnp.zeros((8, 128), F32) for _ in range(16)))
+        for j in range(4):
+            for i in range(4):
+                ref[pl.ds(j * 8 + lead + i, 1), :] = jnp.sum(acc[j * 4 + i], axis=0, keepdims=True)
+
+    def gram(ref, scale, pairs):
+        used = sorted({a for a, _ in pairs} | {e for _, e in pairs})
 
         def block(b, acc):
-            c, r = b // 8, pl.multiple_of((b % 8) * 8, 8)
-            qv = [q[i, c, pl.ds(r, 8), :] for i in range(8)]
-            sv = qv if scale is None else [t * ij[scale, c, pl.ds(r, 8), :] for t in qv]
-            return tuple(acc[n] + sv[a] * qv[e] for n, (a, e) in enumerate(pairs))
-
-        acc = lax.fori_loop(0, 24, block, tuple(jnp.zeros((8, 128), F32) for _ in pairs))
+            c, r = b // 4, pl.multiple_of((b % 4) * 16, 16)
+            out = list(acc)
+            for h in range(2):
+                qv = {i: q[i, c, pl.ds(r + 8 * h, 8), :] for i in used}
+                sv = qv
+                if scale is not None:
+                    weight = ij[scale, c, pl.ds(r + 8 * h, 8), :]
+                    sv = {i: qv[i] * weight for i in {a for a, _ in pairs}}
+                for n, (a, e) in enumerate(pairs):
+                    out[n] = out[n] + sv[a] * qv[e]
+            return tuple(out)
+
+        acc = lax.fori_loop(0, 12, block, tuple(jnp.zeros((8, 128), F32) for _ in pairs))
         for n, (a, e) in enumerate(pairs):
             row = jnp.sum(acc[n], axis=0, keepdims=True)
             ref[pl.ds(a * 8 + e, 1), :] = row
             if a != e:
                 ref[pl.ds(e * 8 + a, 1), :] = row
 
+    def upper(first, second):
+        return [(a, e) for a in first for e in second if a <= e]
+
     def lane_totals(block):
         return jnp.sum(block.T, axis=0, keepdims=True)
 
     def spread(row):
         return jnp.broadcast_to(row * (1.0 / dofs), (128, 128)).T
 
-    def reduce_start(rnd, nr):
-        idx = group(
-            NZ, zpeer, lambda k: rs1.at[rnd, pl.ds(0, nr)], rr1.at[rnd, z, pl.ds(0, nr)]
-        )
-        rr1[rnd, z, pl.ds(0, nr)] = rs1[rnd, pl.ds(0, nr)]
-        return idx
-
-    def reduce_middle(rnd, nr, idx):
-        part = rr1.at[rnd, pl.ds(0, NZ - 1), pl.ds(0, nr)]
-        pltpu.make_async_copy(part, part, rcv.at[idx]).wait()
-        total = rr1[rnd, 0, pl.ds(0, nr)]
-        for k in range(1, NZ):
-            total = total + rr1[rnd, k, pl.ds(0, nr)]
-        rs2[rnd, pl.ds(0, nr)] = total
-        idx2 = group(
-            2 * NP, plane, lambda k: rs2.at[rnd, pl.ds(0, nr)], rr2.at[rnd, pq, pl.ds(0, nr)]
-        )
-        rr2[rnd, pq, pl.ds(0, nr)] = total
-        return idx2
-
-    def reduce_end(rnd, nr, idx):
-        part = rr2.at[rnd, pl.ds(0, 2 * NP - 1), pl.ds(0, nr)]
-        pltpu.make_async_copy(part, part, rcv.at[idx]).wait()
-        total = rr2[rnd, 0, pl.ds(0, nr)]
-        for k in range(1, 2 * NP):
-            total = total + rr2[rnd, k, pl.ds(0, nr)]
-        return total
-
-    def reduce_drain(rnd, nr, idx1, idx2):
-        part = rr1.at[rnd, pl.ds(0, NZ - 1), pl.ds(0, nr)]
-        pltpu.make_async_copy(part, part, snd.at[idx1]).wait()
-        part = rr2.at[rnd, pl.ds(0, 2 * NP - 1), pl.ds(0, nr)]
-        pltpu.make_async_copy(part, part, snd.at[idx2]).wait()
-
-    def exchange_start(s1, r1):
-        idx = group(NZ, zpeer, lambda k: s1.at[(z + k) % NZ], r1.at[z])
-        r1[z] = s1[z]
-        return idx
-
-    def exchange_middle(r1, s2, r2, idx, g):
-        await_group(r1, NZ - 1, idx)
-        for k in range(NP):
-            for e in range(g):
-                s2[k, pl.ds(e * 8, 8), :] = r1[:, e * 8 + k, :]
-        idx2 = group(NP, ppeer, lambda k: s2.at[(p + k) % NP], r2.at[p])
-        r2[p] = s2[p]
-        return idx2
+    def put_rows(planes, e, row):
+        planes[e] = jnp.broadcast_to(row, (NS, 128))
+
+    def row_sum(rbuf, e):
+        return jnp.sum(rbuf[e], axis=0, keepdims=True)
+
+    def own_rows(rbuf, e):
+        return rbuf[e, pl.ds(pl.multiple_of(ri * NS, NS), NS), :]
 
     loads[0].wait()
-    swap_q = send(q.at[pl.ds(0, 4)], q.at[pl.ds(4, 4)], twin)
-    halo_q = send_tangent(q.at[pl.ds(0, 4)], qt.at[:, pl.ds(0, 4)])
+    gather(q, 16)
+    rm[pl.ds(96, 32), :] = jnp.zeros((32, 128), F32)
+    half = (range(0, 4), range(4, 8))
+    gram(rm.at[pl.ds(32, 64)], None, upper(half[0], half[0]))
     loads[1].wait()
-    halo_c = send_tangent(u, ut)
+    gather(u, 0)
+    fold_dots(rm, u, 0)
     loads[2].wait()
-    splat = jnp.full((8, 128), stiff, F32)
-    dgs[0] = jnp.concatenate([dg[48:64, :], splat], axis=0)
-    dgs[1] = jnp.concatenate([dg[0:16, :], splat], axis=0)
-    halo_d = (send(dgs.at[0], dgt.at[0], nxt), send(dgs.at[1], dgt.at[1], prv))
-    dg_edge = jnp.where(ri == 0, dg[pl.ds(15, 4, stride=16), :], dg[pl.ds(0, 4, stride=16), :])
-    pack_radial(u, rsnd.at[0], dg_edge)
-    pack_radial(q, rsnd.at[1], None)
-    side_c = send(rsnd.at[0], ur, across)
-    side_q = send(rsnd.at[1], qr.at[pl.ds(0, 4)], across)
-
-    gather(u, 0)
-    gather(q, 16)
     got = jnp.dot(jnp.concatenate(split2(dg[...]), axis=1), lsm[...], preferred_element_type=F32)
     spare_rows(0, 0, jnp.sum(got * rsm[...], axis=0, keepdims=True))
     spare_rows(0, 1, tgt)
@@ -321,28 +313,43 @@
     for j in range(4):
         spare_rows(16, j, jnp.zeros((1, 512), F32))
     for e in range(2):
-        cs1a[:, pl.ds(e * 8, 8), :] = message(16 * e).reshape(NZ, 8, 128)
-    xa1 = exchange_start(cs1a, cr1a)
+        pa[e] = message(16 * e)
+    splat = jnp.full((8, 128), stiff, F32)
+    dgs[0] = jnp.concatenate([dg[48:64, :], splat], axis=0)
+    dgs[1] = jnp.concatenate([dg[0:16, :], splat], axis=0)
+    dg_edge = jnp.where(ri == 0, dg[pl.ds(15, 4, stride=16), :], dg[pl.ds(0, 4, stride=16), :])
+    pack_radial(u, rsnd.at[0], dg_edge)
+    pack_radial(q, rsnd.at[1], None)
+
+    pl.semaphore_wait(barrier, len(OFFSETS) + 1)
+    swap_q = send(q.at[pl.ds(0, 4)], q.at[pl.ds(4, 4)], twin)
+    touched = exchange(pa, ra, (0, 2), (0, 0))
+    halo_q = send_tangent(q.at[pl.ds(0, 4)], qt.at[:, pl.ds(0, 4)])
+    halo_c = send_tangent(u, ut)
+    halo_d = (send(dgs.at[0], dgt.at[0], nxt), send(dgs.at[1], dgt.at[1], prv))
+    side_c = send(rsnd.at[0], ur, across)
+    side_q = send(rsnd.at[1], qr.at[pl.ds(0, 4)], across)
 
     for j in range(4):
         for c in range(3):
             ij[j, c] = 1.0 / (stiff * 6.0 * kap[c, c] + dg[...] - shf[j])
 
     swap_q.wait_recv()
-    rm[pl.ds(96, 32), :] = jnp.zeros((32, 128), F32)
-    fold_dots(rm, u)
-    gram(rm.at[pl.ds(32, 64)], None)
-    rs1[0, 0] = lane_totals(rm[pl.ds(0, 128), :])
-    ra1 = reduce_start(0, 1)
-
-    for j in range(4):
-        gram(rm.at[pl.ds(128 + j * 64, 64)], j)
-
-    ra2 = reduce_middle(0, 1, ra1)
-    xa2 = exchange_middle(cr1a, cs2a, cr2a, xa1, 2)
-
+    fold_dots(rm, u, 1)
+    gram(rm.at[pl.ds(32, 64)], None, upper(half[0], half[1]))
+    gram(rm.at[pl.ds(32, 64)], None, upper(half[1], half[1]))
+    put_rows(pa, 2, lane_totals(rm[pl.ds(0, 128), :]))
+    summed = exchange(pa, ra, (2, 1), (2, 1))
+
+    def weighted(j, carry):
+        part = rm.at[pl.ds(pl.multiple_of(128 + j * 64, 64), 64)]
+        for a, e in ((0, 0), (0, 1), (1, 1)):
+            gram(part, j, upper(half[a], half[e]))
+        return carry
+
+    lax.fori_loop(0, 4, weighted, 0)
     for e in range(2):
-        rs1[1, 1 + e] = lane_totals(rm[pl.ds(128 + e * 128, 128), :])
+        put_rows(pb, 2 + e, lane_totals(rm[pl.ds(128 + e * 128, 128), :]))
 
     for c in halo_d + halo_q + halo_c + (side_c, side_q):
         c.wait_recv()
@@ -359,9 +366,9 @@
     for j in range(4):
         ijr[j] = 1.0 / (base - shf[j])
 
-    await_group(cr2a, NP - 1, xa2)
-    us[...] = unpack(cr2a[:, pl.ds(0, 8), :].reshape(64, 128))
-    qs[pl.ds(0, 4)] = unpack(cr2a[:, pl.ds(8, 8), :].reshape(64, 128))
+    touched()
+    us[...] = unpack(own_rows(ra, 0))
+    qs[pl.ds(0, 4)] = unpack(own_rows(ra, 1))
     swap_s = send(qs.at[pl.ds(0, 4)], qs.at[pl.ds(4, 4)], twin)
     dv = us[0, 12:16, :]
     sv = us[2, 12:16, :]
@@ -374,13 +381,14 @@
         tr = jnp.floor(tv * (1.0 / 128.0))
         tl = tv - 128.0 * tr
         lanes = slice(sh * 128, (sh + 1) * 128)
-        rtm[:, lanes] = jnp.where(iota((64, 128), 0) == tr, 1.0, 0.0) * kr[sh : sh + 1, :]
+        rtm[:, lanes] = jnp.where(iota((64, 128), 0) == tr, 1.0, 0.0).astype(BF16)
+        krow[pl.ds(sh, 1), :] = kr[sh : sh + 1, :]
         lands = jnp.where(iota((128, 128), 0) == tl, 1.0, 0.0).astype(BF16)
         ltm[:, lanes] = lands
         ltm[:, 512 + sh * 128 : 640 + sh * 128] = lands
 
-    total = reduce_end(0, 1, ra2)
-    wide = spread(total[0])
+    summed()
+    wide = spread(row_sum(ra, 2))
     acf[...] = wide[0:32].reshape(4, 8, 128)
     st_s[...] = wide[32:96].reshape(8, 8, 128)
 
@@ -453,18 +461,22 @@
     edge = row_in == 15 * (1 - ri)
 
     def apply(dref):
+        def forces(j, carry):
+            base = pl.multiple_of(j * 192, 192)
+            for c in range(3):
+                for sh in range(4):
+                    v = us[j, pl.ds(c * 4 + sh, 1), :] * krow[pl.ds(sh, 1), :]
+                    vh = v.astype(BF16).astype(F32)
+                    mask = rtm[:, sh * 128 : (sh + 1) * 128]
+                    for e, part in enumerate((vh, v - vh)):
+                        full = jnp.broadcast_to(part, (64, 128)).astype(BF16)
+                        amat[pl.ds(base + c * 64, 64), pl.ds(e * 512 + sh * 128, 128)] = mask * full
+            return carry
+
+        lax.fori_loop(0, 4, forces, 0)
+        land[...] = lax.dot_general(amat[...], ltm[...], NT, preferred_element_type=F32)
+
         def column(j, carry):
-            hs = []
-            for c in range(3):
-                hrow, lrow = [], []
-                for sh in range(4):
-                    v = us[j, pl.ds(c * 4 + sh, 1), :]
-                    a = rtm[:, sh * 128 : (sh + 1) * 128] * v
-                    ah, al = split2(a)
-                    hrow.append(ah)
-                    lrow.append(al)
-                hs.append(jnp.concatenate(hrow + lrow, axis=1))
-            touch = lax.dot_general(jnp.concatenate(hs, axis=0), ltm[...], NT, preferred_element_type=F32)
             xs = [u[j, c] for c in range(3)]
             for c in range(3):
                 v = xs[c]
@@ -483,7 +495,8 @@
                 for e in range(3):
                     if e != c:
                         mixed = mixed + kap[c, e] * xs[e]
-                out = stiff * mixed + (dg[...] - shf[j]) * v + touch[c * 64 : (c + 1) * 64]
+                out = stiff * mixed + (dg[...] - shf[j]) * v
+                out = out + land[pl.ds(pl.multiple_of(j * 192, 192) + c * 64, 64), :]
                 w[j, c] = out
                 dref[j, c] = -(rho[j, c] + out) * ij[j, c]
             return carry
@@ -510,41 +523,33 @@
                 acf[j] = a + DAMPING * (e - se)
 
     loads[3].wait()
-    drains = []
     for rnd in range(3):
         last = rnd == 2
-        nr = 3 if rnd == 0 else 1
         dref = d.at[rnd]
+        planes, rbuf = ((pb, rb), (pc, rc), (pd, rd))[rnd]
         apply(dref)
         if not last:
             pack_radial(dref, rsnd.at[2 + rnd], None)
-            halo = send_tangent(dref, dt.at[rnd])
-            side = send(rsnd.at[2 + rnd], dr.at[rnd], across)
+            halo = send_tangent(dref, dt.at[rnd]) + (send(rsnd.at[2 + rnd], dr.at[rnd], across),)
             gather(dref, 0)
-            cs1[rnd] = message(0).reshape(NZ, 8, 128)
-            x1 = exchange_start(cs1.at[rnd], cr1.at[rnd])
-        fold_dots(rm, w)
-        fold_dots(rm.at[pl.ds(32, 32)], dref)
-        rs1[rnd + 1, 0] = lane_totals(rm[pl.ds(0, 128), :])
-        r1 = reduce_start(rnd + 1, nr)
+            planes[0] = message(0)
+        for e in range(2):
+            fold_dots(rm, w, e)
+            fold_dots(rm.at[pl.ds(32, 32)], dref, e)
+        put_rows(planes, 1, lane_totals(rm[pl.ds(0, 128), :]))
+        nr = 3 if rnd == 0 else 1
+        arrived = exchange(planes, rbuf, (1, 1) if last else (0, 1 + nr), (1, nr))
         if not last:
-            x2 = None
-        r2 = reduce_middle(rnd + 1, nr, r1)
-        drains.append((rnd + 1, nr, r1, r2))
-        if not last:
-            x2 = exchange_middle(cr1.at[rnd], cs2.at[rnd], cr2.at[rnd], x1, 1)
-            for c in halo + (side,):
+            for c in halo:
                 c.wait_recv()
-        total = reduce_end(rnd + 1, nr, r2)
+        arrived()
         if rnd == 0:
             for e in range(2):
-                mt_s[pl.ds(2 * e, 2)] = spread(total[1 + e]).reshape(2, 8, 8, 128)
-        coefficients(total[0], last)
+                mt_s[pl.ds(2 * e, 2)] = spread(row_sum(rbuf, 2 + e)).reshape(2, 8, 8, 128)
+        coefficients(row_sum(rbuf, 1), last)
         if not last:
-            await_group(cr2.at[rnd], NP - 1, x2)
-            ds[rnd] = unpack(cr2[rnd].reshape(64, 128))
+            ds[rnd] = unpack(own_rows(rbuf, 0))
             update(rnd)
-            drains.append((rnd, x1, x2))
 
     def finish(b, carry):
         c, r = b // 4, pl.multiple_of((b % 4) * 16, 16)
@@ -566,15 +571,8 @@
         c.start()
     for c in pending:
         c.wait_send()
-    drain_group(cr1a, NZ - 1, xa1)
-    drain_group(cr2a, NP - 1, xa2)
-    reduce_drain(0, 1, ra1, ra2)
-    for t in drains:
-        if len(t) == 4:
-            reduce_drain(*t)
-        else:
-            drain_group(cr1.at[t[0]], NZ - 1, t[1])
-            drain_group(cr2.at[t[0]], NP - 1, t[2])
+    for wait in drains:
+        wait()
     for c in outs:
         c.wait()
 
@@ -598,11 +596,11 @@
         vm((2,) + sheet, F32), vm((2, 2) + sheet, F32),
         vm(small, F32), vm((8, 16, 128), F32), vm(small, F32), vm((2,) + small, F32),
         vm(small, F32), vm((8, 16, 128), F32), vm(small, F32), vm((2,) + small, F32), vm((4,) + small, F32),
-        vm((256, 512), BF16), vm((64, 512), F32), vm((128, 1024), BF16), vm((64, 512), F32), vm((32, 4, 128), F32),
-        vm((NZ, 16, 128), F32), vm((NZ, 16, 128), F32), vm((NP, 16, 128), F32), vm((NP, 16, 128), F32),
-        vm((2, NZ, 8, 128), F32), vm((2, NZ, 8, 128), F32), vm((2, NP, 8, 128), F32), vm((2, NP, 8, 128), F32),
-        vm((384, 128), F32), vm((4, 3, 1, 128), F32), vm((4, NZ, 3, 1, 128), F32), vm((4, 3, 1, 128), F32),
-        vm((4, 2 * NP, 3, 1, 128), F32),
+        vm((256, 512), BF16), vm((64, 512), F32), vm((128, 1024), BF16), vm((64, 512), BF16), vm((32, 4, 128), F32),
+        vm((768, 1024), BF16), vm((768, 128), F32), vm((8, 128), F32),
+        vm((3, 64, 128), F32), vm((3, 128, 128), F32), vm((4, 64, 128), F32), vm((4, 128, 128), F32),
+        vm((2, 64, 128), F32), vm((2, 128, 128), F32), vm((2, 64, 128), F32), vm((2, 128, 128), F32),
+        vm((384, 128), F32),
         vm((2, 4, 8, 128), F32), vm((8, 8, 128), F32), vm((4, 8, 8, 128), F32), vm((4, 8, 128), F32),
         pltpu.SemaphoreType.DMA((4,)), pltpu.SemaphoreType.DMA((2,)),
         pltpu.SemaphoreType.DMA((36,)), pltpu.SemaphoreType.DMA((36,)),

time: 70.8 us -> 66.2 us (0.935)
  Pallas kernels: 67.1 us -> 62.5 us
    pallas_call x1, Pallas kernels: 67.1 us -> 62.5 us  [body(): pl.pallas_call(functools.partial(kernel, dofs), out_shape=(jax.ShapeDtype...]
where the time goes in v1:
time: 66.2 us; the launch traced here: 66.1 us
  Pallas kernels  62.5 us (94%)
  local copies, waits for them, and re-layouts  2.2 us (3%)
  between operations  1.35 us (2%)
    pallas_call x1, Pallas kernels, body(): pl.pallas_call(functools.partial(kernel, dofs), out_shape=(jax.ShapeDtype...  62.5 us
    unnamed x16, local copies, waits for them, and re-layouts  2.2 us

profile of v1, /device:TPU:2, one launch (start us, length us, event | category | flops | bytes accessed | tf_op | source)
XLA Modules:
  0.0 66.1 jit_solution(9200808174231838932)
XLA Ops:
  1.3 0.0 copy-start.4
  1.3 0.0 copy-start.6
  1.3 0.0 copy-start.2
  1.3 0.0 copy-start.3
  1.3 0.0 copy-start
  1.3 0.0 copy-start.1
  1.3 0.0 copy-start.5
  1.3 0.6 copy-done.4
  2.0 0.0 copy-done.6
  2.0 0.0 copy-done.2
  2.0 0.0 copy-done.3
  2.0 0.0 copy-done
  2.0 0.0 copy-done.1
  2.0 0.0 copy-done.5
  2.0 62.5 %sweeps.1 = (f32[4,3,64,128]{3,2,1,0:T(8,128)S(1)}, f32[4,3,64,128]{3,2,1,0:T(8,128)S(1)}) custom-call(s32[2,128]{1,0:T(2,128)S(1)} %bitcast.12, s32[2,128]{1,0:T(2,128)S(1)} %bitcast.13, s32[2,128]{1,0:T(2,128)S(1)} %bitcast.14, f32[2,128]{1,0:T(2,128)S(1)} %bitcast.15, f32[3,3]{1,0:T(4,128)S(1)} %copy-done, s32[1]{0:T(128)S(6)} %copy.16.cid, ...), custom_call_target="tpu_custom_call" | custom-call | tf_op jit(solution)/shard_map/sweeps/pallas_call | solution.py:610
  64.6 0.7 %copy.17 = f32[4,3,4,16,128]{4,3,2,1,0:T(8,128)} copy(f32[4,3,4,16,128]{4,3,2,1,0:T(8,128)S(1)} %bitcast.11) | data formatting | bytes 786432
  65.3 0.7 %copy.18 = f32[4,3,4,16,128]{4,3,2,1,0:T(8,128)} copy(f32[4,3,4,16,128]{4,3,2,1,0:T(8,128)S(1)} %bitcast.10) | data formatting | bytes 786432
Async XLA Ops:
  1.3 0.7 %copy-start.4 = (f32[256]{0:T(256)S(1)}, f32[256]{0:T(256)}, u32[]{:S(2)}) copy-start(f32[256]{0:T(256)} %param.23) | copy-start | bytes 3076
  1.3 0.7 %copy-start.6 = (f32[4]{0:T(128)S(1)}, f32[4]{0:T(128)}, u32[]{:S(2)}) copy-start(f32[4]{0:T(128)} %shf.1) | copy-start | bytes 52
  1.3 0.7 %copy-start.2 = (s32[256]{0:T(256)S(1)}, s32[256]{0:T(256)}, u32[]{:S(2)}) copy-start(s32[256]{0:T(256)} %param.21) | copy-start | bytes 3076
  1.3 0.7 %copy-start.3 = (s32[256]{0:T(256)S(1)}, s32[256]{0:T(256)}, u32[]{:S(2)}) copy-start(s32[256]{0:T(256)} %param.22) | copy-start | bytes 3076
  1.3 0.7 %copy-start = (f32[3,3]{1,0:T(4,128)S(1)}, f32[3,3]{1,0:T(4,128)}, u32[]{:S(2)}) copy-start(f32[3,3]{1,0:T(4,128)} %kap.1) | copy-start | bytes 112
  1.3 0.7 %copy-start.1 = (s32[256,1]{0,1:T(1,128)S(1)}, s32[256,1]{0,1:T(1,128)}, u32[]{:S(2)}) copy-start(s32[256,1]{0,1:T(1,128)} %param.20) | copy-start | bytes 3076
  1.3 0.7 %copy-start.5 = (f32[8]{0:T(128)S(1)}, f32[8]{0:T(128)}, u32[]{:S(2)}) copy-start(f32[8]{0:T(128)} %cst.1) | copy-start | bytes 100

commit v2 on v1

--- a/solution.py
+++ b/solution.py
@@ -58,7 +58,7 @@
     pa, ra, pb, rb, pc, rc, pd, rd,
     rm,
     cf, st_s, mt_s, acf,
-    ld_sem, out_sem, snd, rcv,
+    ld_sem, snd, rcv,
 ):
     x = lax.axis_index("sector_0")
     y = lax.axis_index("sector_1")
@@ -95,10 +95,6 @@
     def sig(dev):
         pl.semaphore_signal(barrier, inc=1, device_id=dev, device_id_type=MESH_ID)
 
-    for offset in OFFSETS:
-        sig(peer(offset))
-    sig(twin)
-
     loads = [
         pltpu.make_async_copy(q_h, q.at[pl.ds(0, 4)], ld_sem.at[0]),
         pltpu.make_async_copy(c0_h, u, ld_sem.at[1]),
@@ -108,13 +104,17 @@
     for c in loads:
         c.start()
 
+    for offset in OFFSETS:
+        sig(peer(offset))
+    sig(twin)
+
     count = [0]
     pending = []
 
-    def rcopy(src, dst, dev, idx):
+    def rcopy(src, dst, dev, idx, kind=MESH_ID):
         return pltpu.make_async_remote_copy(
             src_ref=src, dst_ref=dst, send_sem=snd.at[idx], recv_sem=rcv.at[idx],
-            device_id=dev, device_id_type=MESH_ID,
+            device_id=dev, device_id_type=kind,
         )
 
     def send(src, dst, dev):
@@ -239,18 +239,17 @@
     def fold_dots(ref, vref, half):
         lead = half * 4
 
-        def block(b, acc):
-            c, r = b // 4, pl.multiple_of((b % 4) * 16, 16)
+        def block(c, acc):
             out = list(acc)
-            for e in range(2):
-                qv = [q[lead + i, c, pl.ds(r + 8 * e, 8), :] for i in range(4)]
-                vv = [vref[j, c, pl.ds(r + 8 * e, 8), :] for j in range(4)]
+            for e in range(8):
+                qv = [q[lead + i, c, 8 * e : 8 * e + 8, :] for i in range(4)]
+                vv = [vref[j, c, 8 * e : 8 * e + 8, :] for j in range(4)]
                 for j in range(4):
                     for i in range(4):
                         out[j * 4 + i] = out[j * 4 + i] + qv[i] * vv[j]
             return tuple(out)
 
-        acc = lax.fori_loop(0, 12, block, tuple(jnp.zeros((8, 128), F32) for _ in range(16)))
+        acc = lax.fori_loop(0, 3, block, tuple(jnp.zeros((8, 128), F32) for _ in range(16)))
         for j in range(4):
             for i in range(4):
                 ref[pl.ds(j * 8 + lead + i, 1), :] = jnp.sum(acc[j * 4 + i], axis=0, keepdims=True)
@@ -259,9 +258,9 @@
         used = sorted({a for a, _ in pairs} | {e for _, e in pairs})
 
         def block(b, acc):
-            c, r = b // 4, pl.multiple_of((b % 4) * 16, 16)
+            c, r = b // 2, pl.multiple_of((b % 2) * 32, 32)
             out = list(acc)
-            for h in range(2):
+            for h in range(4):
                 qv = {i: q[i, c, pl.ds(r + 8 * h, 8), :] for i in used}
                 sv = qv
                 if scale is not None:
@@ -271,7 +270,7 @@
                     out[n] = out[n] + sv[a] * qv[e]
             return tuple(out)
 
-        acc = lax.fori_loop(0, 12, block, tuple(jnp.zeros((8, 128), F32) for _ in pairs))
+        acc = lax.fori_loop(0, 6, block, tuple(jnp.zeros((8, 128), F32) for _ in pairs))
         for n, (a, e) in enumerate(pairs):
             row = jnp.sum(acc[n], axis=0, keepdims=True)
             ref[pl.ds(a * 8 + e, 1), :] = row
@@ -324,11 +323,7 @@
     pl.semaphore_wait(barrier, len(OFFSETS) + 1)
     swap_q = send(q.at[pl.ds(0, 4)], q.at[pl.ds(4, 4)], twin)
     touched = exchange(pa, ra, (0, 2), (0, 0))
-    halo_q = send_tangent(q.at[pl.ds(0, 4)], qt.at[:, pl.ds(0, 4)])
     halo_c = send_tangent(u, ut)
-    halo_d = (send(dgs.at[0], dgt.at[0], nxt), send(dgs.at[1], dgt.at[1], prv))
-    side_c = send(rsnd.at[0], ur, across)
-    side_q = send(rsnd.at[1], qr.at[pl.ds(0, 4)], across)
 
     for j in range(4):
         for c in range(3):
@@ -340,6 +335,10 @@
     gram(rm.at[pl.ds(32, 64)], None, upper(half[1], half[1]))
     put_rows(pa, 2, lane_totals(rm[pl.ds(0, 128), :]))
     summed = exchange(pa, ra, (2, 1), (2, 1))
+    halo_q = send_tangent(q.at[pl.ds(0, 4)], qt.at[:, pl.ds(0, 4)])
+    halo_d = (send(dgs.at[0], dgt.at[0], nxt), send(dgs.at[1], dgt.at[1], prv))
+    side_c = send(rsnd.at[0], ur, across)
+    side_q = send(rsnd.at[1], qr.at[pl.ds(0, 4)], across)
 
     def weighted(j, carry):
         part = rm.at[pl.ds(pl.multiple_of(128 + j * 64, 64), 64)]
@@ -432,8 +431,8 @@
 
             lax.fori_loop(0, blocks, step, 0)
 
-    def update(rnd):
-        for n in range(4):
+    def update(rnd, which):
+        for n in which:
             blocks, place, get, (ru, rq, rj, rd) = regions[n]
 
             def step(b, carry):
@@ -464,13 +463,16 @@
         def forces(j, carry):
             base = pl.multiple_of(j * 192, 192)
             for c in range(3):
+                vs = us[j, c * 4 : c * 4 + 4, :] * krow[0:4, :]
+                vh = vs.astype(BF16).astype(F32)
                 for sh in range(4):
-                    v = us[j, pl.ds(c * 4 + sh, 1), :] * krow[pl.ds(sh, 1), :]
-                    vh = v.astype(BF16).astype(F32)
                     mask = rtm[:, sh * 128 : (sh + 1) * 128]
-                    for e, part in enumerate((vh, v - vh)):
-                        full = jnp.broadcast_to(part, (64, 128)).astype(BF16)
-                        amat[pl.ds(base + c * 64, 64), pl.ds(e * 512 + sh * 128, 128)] = mask * full
+                    for e, part in enumerate((vh, vs - vh)):
+                        full = jnp.broadcast_to(part[sh : sh + 1, :], (16, 128)).astype(BF16)
+                        for t in range(4):
+                            amat[pl.ds(base + c * 64 + 16 * t, 16), pl.ds(e * 512 + sh * 128, 128)] = (
+                                mask[16 * t : 16 * t + 16] * full
+                            )
             return carry
 
         lax.fori_loop(0, 4, forces, 0)
@@ -528,28 +530,31 @@
         dref = d.at[rnd]
         planes, rbuf = ((pb, rb), (pc, rc), (pd, rd))[rnd]
         apply(dref)
-        if not last:
-            pack_radial(dref, rsnd.at[2 + rnd], None)
-            halo = send_tangent(dref, dt.at[rnd]) + (send(rsnd.at[2 + rnd], dr.at[rnd], across),)
-            gather(dref, 0)
-            planes[0] = message(0)
         for e in range(2):
             fold_dots(rm, w, e)
             fold_dots(rm.at[pl.ds(32, 32)], dref, e)
         put_rows(planes, 1, lane_totals(rm[pl.ds(0, 128), :]))
         nr = 3 if rnd == 0 else 1
-        arrived = exchange(planes, rbuf, (1, 1) if last else (0, 1 + nr), (1, nr))
+        summed = exchange(planes, rbuf, (1, nr), (1, nr))
         if not last:
-            for c in halo:
-                c.wait_recv()
-        arrived()
+            gather(dref, 0)
+            planes[0] = message(0)
+            touched = exchange(planes, rbuf, (0, 1), (0, 0))
+            pack_radial(dref, rsnd.at[2 + rnd], None)
+            halo = send_tangent(dref, dt.at[rnd]) + (send(rsnd.at[2 + rnd], dr.at[rnd], across),)
+        summed()
         if rnd == 0:
             for e in range(2):
                 mt_s[pl.ds(2 * e, 2)] = spread(row_sum(rbuf, 2 + e)).reshape(2, 8, 8, 128)
         coefficients(row_sum(rbuf, 1), last)
         if not last:
+            update(rnd, (0,))
+            for c in halo:
+                c.wait_recv()
+            update(rnd, (1, 3))
+            touched()
             ds[rnd] = unpack(own_rows(rbuf, 0))
-            update(rnd)
+            update(rnd, (2,))
 
     def finish(b, carry):
         c, r = b // 4, pl.multiple_of((b % 4) * 16, 16)
@@ -558,23 +563,27 @@
         for j in range(4):
             res = mix(cf.at[0], j, qv) - rho[j, c, pl.ds(r, 16), :] - w[j, c, pl.ds(r, 16), :]
             new = u[j, c, pl.ds(r, 16), :] + DAMPING * res * ij[j, c, pl.ds(r, 16), :] + mix(cf.at[1], j, qv)
-            w[j, c, pl.ds(r, 16), :] = res
-            rho[j, c, pl.ds(r, 16), :] = new
+            or_h[j, c, pl.ds(r, 16), :] = res
+            oc_h[j, c, pl.ds(r, 16), :] = new
         return carry
 
     lax.fori_loop(0, 12, finish, 0)
-    outs = [
-        pltpu.make_async_copy(rho, oc_h, out_sem.at[0]),
-        pltpu.make_async_copy(w, or_h, out_sem.at[1]),
-    ]
-    for c in outs:
-        c.start()
     for c in pending:
         c.wait_send()
     for wait in drains:
         wait()
-    for c in outs:
+
+
+def store(a, b, out_a, out_b, sem):
+    copies = [pltpu.make_async_copy(a, out_a, sem.at[0]), pltpu.make_async_copy(b, out_b, sem.at[1])]
+    for c in copies:
+        c.start()
+    for c in copies:
         c.wait()
+
+
+def in_hbm(a):
+    return pltpu.with_memory_space_constraint(a, pltpu.HBM)
 
 
 def body(
@@ -602,7 +611,7 @@
         vm((2, 64, 128), F32), vm((2, 128, 128), F32), vm((2, 64, 128), F32), vm((2, 128, 128), F32),
         vm((384, 128), F32),
         vm((2, 4, 8, 128), F32), vm((8, 8, 128), F32), vm((4, 8, 8, 128), F32), vm((4, 8, 128), F32),
-        pltpu.SemaphoreType.DMA((4,)), pltpu.SemaphoreType.DMA((2,)),
+        pltpu.SemaphoreType.DMA((4,)),
         pltpu.SemaphoreType.DMA((36,)), pltpu.SemaphoreType.DMA((36,)),
     ]
     anyspace = pl.BlockSpec(memory_space=pl.ANY)
@@ -610,19 +619,26 @@
     correction, residual = pl.pallas_call(
         functools.partial(kernel, dofs),
         out_shape=(jax.ShapeDtypeStruct(flat, F32), jax.ShapeDtypeStruct(flat, F32)),
-        in_specs=[pl.BlockSpec(memory_space=pltpu.VMEM)] * 4 + [smem] * 4 + [pl.BlockSpec(memory_space=pltpu.HBM)] * 4,
-        out_specs=(anyspace, anyspace),
+        in_specs=[pl.BlockSpec(memory_space=pltpu.VMEM)] * 4 + [smem] * 4 + [anyspace] * 4,
+        out_specs=(pl.BlockSpec(memory_space=pltpu.VMEM),) * 2,
         scratch_shapes=scratch,
         compiler_params=pltpu.CompilerParams(collective_id=0, has_side_effects=True, vmem_limit_bytes=16 * 1024 * 1024),
         name="sweeps",
     )(
         contact_dest.reshape(2, 128), contact_source.reshape(2, 128), contact_target.reshape(2, 128),
         contact_stiffness.reshape(2, 128), coupling, class_ids, class_stiffness, shifts,
-        *(pltpu.with_memory_space_constraint(a, pltpu.HBM) for a in (
-            correction_guess.reshape(flat), ritz_residual.reshape(flat), ritz_basis.reshape(flat),
-            diagonal.reshape(tang * rloc, ax),
-        )),
+        in_hbm(correction_guess.reshape(flat)), in_hbm(ritz_residual.reshape(flat)),
+        in_hbm(ritz_basis.reshape(flat)), in_hbm(diagonal.reshape(tang * rloc, ax)),
     )
+    correction, residual = pl.pallas_call(
+        store,
+        out_shape=(jax.ShapeDtypeStruct(flat, F32), jax.ShapeDtypeStruct(flat, F32)),
+        in_specs=[anyspace] * 2,
+        out_specs=(anyspace, anyspace),
+        scratch_shapes=[pltpu.SemaphoreType.DMA((2,))],
+        compiler_params=pltpu.CompilerParams(vmem_limit_bytes=1024 * 1024),
+        name="store",
+    )(correction, residual)
     shape = correction_guess.shape
     return correction.reshape(shape), residual.reshape(shape)
 

time: 66.2 us -> 61.5 us (0.929)
  Pallas kernels: 62.5 us -> 59.2 us
  local copies, waits for them, and re-layouts: 2.2 us -> 0.7 us
    pallas_call x1, Pallas kernels: 62.5 us -> 58.3 us  [body(): pl.pallas_call(functools.partial(kernel, dofs), out_shape=(jax.ShapeDtype...]
    unnamed x16 -> x14, local copies, waits for them, and re-layouts: 2.2 us -> 0.7 us
    pallas_call x0 -> x1, Pallas kernels: none -> 0.89 us  [body(): pl.pallas_call(store, out_shape=(jax.ShapeDtypeStruct(flat, F32), jax.Sha...]
where the time goes in v2:
time: 61.5 us; the launch traced here: 61.2 us
  Pallas kernels  59.2 us (96%)
  between operations  1.35 us (2%)
  local copies, waits for them, and re-layouts  0.7 us (1%)
    pallas_call x1, Pallas kernels, body(): pl.pallas_call(functools.partial(kernel, dofs), out_shape=(jax.ShapeDtype...  58.3 us

profile of v2, /device:TPU:2, one launch (start us, length us, event | category | flops | bytes accessed | tf_op | source)
XLA Modules:
  0.0 61.2 jit_solution(15400156183189140057)
XLA Ops:
  1.3 0.0 copy-start.4
  1.3 0.0 copy-start.6
  1.3 0.0 copy-start.2
  1.3 0.0 copy-start.3
  1.3 0.0 copy-start
  1.3 0.0 copy-start.1
  1.3 0.0 copy-start.5
  1.3 0.6 copy-done.4
  2.0 0.0 copy-done.6
  2.0 0.0 copy-done.2
  2.0 0.0 copy-done.3
  2.0 0.0 copy-done
  2.0 0.0 copy-done.1
  2.0 0.0 copy-done.5
  2.0 58.3 %sweeps.1 = (f32[4,3,64,128]{3,2,1,0:T(8,128)S(1)}, f32[4,3,64,128]{3,2,1,0:T(8,128)S(1)}) custom-call(s32[2,128]{1,0:T(2,128)S(1)} %bitcast.10, s32[2,128]{1,0:T(2,128)S(1)} %bitcast.11, s32[2,128]{1,0:T(2,128)S(1)} %bitcast.12, f32[2,128]{1,0:T(2,128)S(1)} %bitcast.13, f32[3,3]{1,0:T(4,128)S(1)} %copy-done, s32[1]{0:T(128)S(6)} %copy.14.cid, ...), custom_call_target="tpu_custom_call" | custom-call | tf_op jit(solution)/shard_map/sweeps/pallas_call | solution.py:619
  60.3 0.9 %store.1 = (f32[4,3,64,128]{3,2,1,0:T(8,128)}, f32[4,3,64,128]{3,2,1,0:T(8,128)}) custom-call(f32[4,3,64,128]{3,2,1,0:T(8,128)S(1)} %get-tuple-element.6.a, f32[4,3,64,128]{3,2,1,0:T(8,128)S(1)} %get-tuple-element.7.b), custom_call_target="tpu_custom_call" | custom-call | tf_op jit(solution)/shard_map/store/pallas_call | solution.py:633
Async XLA Ops:
  1.3 0.7 %copy-start.4 = (f32[256]{0:T(256)S(1)}, f32[256]{0:T(256)}, u32[]{:S(2)}) copy-start(f32[256]{0:T(256)} %param.23) | copy-start | bytes 3076
  1.3 0.7 %copy-start.6 = (f32[4]{0:T(128)S(1)}, f32[4]{0:T(128)}, u32[]{:S(2)}) copy-start(f32[4]{0:T(128)} %shf.1) | copy-start | bytes 52
  1.3 0.7 %copy-start.2 = (s32[256]{0:T(256)S(1)}, s32[256]{0:T(256)}, u32[]{:S(2)}) copy-start(s32[256]{0:T(256)} %param.21) | copy-start | bytes 3076
  1.3 0.7 %copy-start.3 = (s32[256]{0:T(256)S(1)}, s32[256]{0:T(256)}, u32[]{:S(2)}) copy-start(s32[256]{0:T(256)} %param.22) | copy-start | bytes 3076
  1.3 0.7 %copy-start = (f32[3,3]{1,0:T(4,128)S(1)}, f32[3,3]{1,0:T(4,128)}, u32[]{:S(2)}) copy-start(f32[3,3]{1,0:T(4,128)} %kap.1) | copy-start | bytes 112
  1.3 0.7 %copy-start.1 = (s32[256,1]{0,1:T(1,128)S(1)}, s32[256,1]{0,1:T(1,128)}, u32[]{:S(2)}) copy-start(s32[256,1]{0,1:T(1,128)} %param.20) | copy-start | bytes 3076
  1.3 0.7 %copy-start.5 = (f32[8]{0:T(128)S(1)}, f32[8]{0:T(128)}, u32[]{:S(2)}) copy-start(f32[8]{0:T(128)} %cst.1) | copy-start | bytes 100

commit v3 on v2

--- a/solution.py
+++ b/solution.py
@@ -323,7 +323,8 @@
     pl.semaphore_wait(barrier, len(OFFSETS) + 1)
     swap_q = send(q.at[pl.ds(0, 4)], q.at[pl.ds(4, 4)], twin)
     touched = exchange(pa, ra, (0, 2), (0, 0))
-    halo_c = send_tangent(u, ut)
+    halo_q = send_tangent(q.at[pl.ds(0, 4)], qt.at[:, pl.ds(0, 4)])
+    side_q = send(rsnd.at[1], qr.at[pl.ds(0, 4)], across)
 
     for j in range(4):
         for c in range(3):
@@ -335,10 +336,9 @@
     gram(rm.at[pl.ds(32, 64)], None, upper(half[1], half[1]))
     put_rows(pa, 2, lane_totals(rm[pl.ds(0, 128), :]))
     summed = exchange(pa, ra, (2, 1), (2, 1))
-    halo_q = send_tangent(q.at[pl.ds(0, 4)], qt.at[:, pl.ds(0, 4)])
+    side_c = send(rsnd.at[0], ur, across)
     halo_d = (send(dgs.at[0], dgt.at[0], nxt), send(dgs.at[1], dgt.at[1], prv))
-    side_c = send(rsnd.at[0], ur, across)
-    side_q = send(rsnd.at[1], qr.at[pl.ds(0, 4)], across)
+    halo_c = send_tangent(u, ut)
 
     def weighted(j, carry):
         part = rm.at[pl.ds(pl.multiple_of(128 + j * 64, 64), 64)]
@@ -350,10 +350,12 @@
     for e in range(2):
         put_rows(pb, 2 + e, lane_totals(rm[pl.ds(128 + e * 128, 128), :]))
 
-    for c in halo_d + halo_q + halo_c + (side_c, side_q):
+    for c in halo_q + (side_q,):
         c.wait_recv()
     swap_t = send(qt.at[:, pl.ds(0, 4)], qt.at[:, pl.ds(4, 4)], twin)
     swap_r = send(qr.at[pl.ds(0, 4)], qr.at[pl.ds(4, 4)], twin)
+    for c in halo_d + halo_c + (side_c,):
+        c.wait_recv()
     for side in range(2):
         sv = jnp.concatenate([dgt[side, 16:24, :], dgt[side, 16:24, :]], axis=0)
         dv = dgt[side, 0:16, :]
@@ -455,8 +457,8 @@
     swap_s.wait_recv()
     first_update((1, 2, 3))
 
-    row_in = lax.broadcasted_iota(jnp.int32, (64, 128), 0) % 16
-    lane_in = lax.broadcasted_iota(jnp.int32, (64, 128), 1)
+    row_in = lax.broadcasted_iota(jnp.int32, (16, 128), 0)
+    lane_in = lax.broadcasted_iota(jnp.int32, (16, 128), 1)
     edge = row_in == 15 * (1 - ri)
 
     def apply(dref):
@@ -479,28 +481,29 @@
         land[...] = lax.dot_general(amat[...], ltm[...], NT, preferred_element_type=F32)
 
         def column(j, carry):
-            xs = [u[j, c] for c in range(3)]
-            for c in range(3):
-                v = xs[c]
-                before = jnp.concatenate([ut[0, j, c], v[0:48]], axis=0)
-                after = jnp.concatenate([v[16:64], ut[1, j, c]], axis=0)
-                lap = 6.0 * v - before - after
-                lap = lap - jnp.where(row_in == 0, 0.0, pltpu.roll(v, 1, 0))
-                lap = lap - jnp.where(row_in == 15, 0.0, pltpu.roll(v, 63, 0))
-                beside = jnp.concatenate(
-                    [jnp.broadcast_to(ur[j, pl.ds(c * 4 + t, 1), :], (16, 128)) for t in range(4)], axis=0
-                )
-                lap = lap - jnp.where(edge, beside, 0.0)
-                lap = lap - jnp.where(lane_in == 0, 0.0, pltpu.roll(v, 1, 1))
-                lap = lap - jnp.where(lane_in == 127, 0.0, pltpu.roll(v, 127, 1))
-                mixed = kap[c, c] * lap
-                for e in range(3):
-                    if e != c:
-                        mixed = mixed + kap[c, e] * xs[e]
-                out = stiff * mixed + (dg[...] - shf[j]) * v
-                out = out + land[pl.ds(pl.multiple_of(j * 192, 192) + c * 64, 64), :]
-                w[j, c] = out
-                dref[j, c] = -(rho[j, c] + out) * ij[j, c]
+            for t in range(4):
+                slab = slice(16 * t, 16 * t + 16)
+                xs = [u[j, c, slab, :] for c in range(3)]
+                base = dg[slab, :] - shf[j]
+                for c in range(3):
+                    v = xs[c]
+                    before = ut[0, j, c] if t == 0 else u[j, c, 16 * t - 16 : 16 * t, :]
+                    after = ut[1, j, c] if t == 3 else u[j, c, 16 * t + 16 : 16 * t + 32, :]
+                    lap = 6.0 * v - before - after
+                    lap = lap - jnp.where(row_in == 0, 0.0, pltpu.roll(v, 1, 0))
+                    lap = lap - jnp.where(row_in == 15, 0.0, pltpu.roll(v, 15, 0))
+                    beside = jnp.broadcast_to(ur[j, c * 4 + t : c * 4 + t + 1, :], (16, 128))
+                    lap = lap - jnp.where(edge, beside, 0.0)
+                    lap = lap - jnp.where(lane_in == 0, 0.0, pltpu.roll(v, 1, 1))
+                    lap = lap - jnp.where(lane_in == 127, 0.0, pltpu.roll(v, 127, 1))
+                    mixed = kap[c, c] * lap
+                    for e in range(3):
+                        if e != c:
+                            mixed = mixed + kap[c, e] * xs[e]
+                    out = stiff * mixed + base * v
+                    out = out + land[pl.ds(pl.multiple_of(j * 192, 192) + c * 64 + 16 * t, 16), :]
+                    w[j, c, slab, :] = out
+                    dref[j, c, slab, :] = -(rho[j, c, slab, :] + out) * ij[j, c, slab, :]
             return carry
 
         lax.fori_loop(0, 4, column, 0)
@@ -625,8 +628,9 @@
         compiler_params=pltpu.CompilerParams(collective_id=0, has_side_effects=True, vmem_limit_bytes=16 * 1024 * 1024),
         name="sweeps",
     )(
-        contact_dest.reshape(2, 128), contact_source.reshape(2, 128), contact_target.reshape(2, 128),
-        contact_stiffness.reshape(2, 128), coupling, class_ids, class_stiffness, shifts,
+        in_hbm(contact_dest.reshape(2, 128)), in_hbm(contact_source.reshape(2, 128)),
+        in_hbm(contact_target.reshape(2, 128)), in_hbm(contact_stiffness.reshape(2, 128)),
+        in_hbm(coupling), class_ids, in_hbm(class_stiffness), in_hbm(shifts),
         in_hbm(correction_guess.reshape(flat)), in_hbm(ritz_residual.reshape(flat)),
         in_hbm(ritz_basis.reshape(flat)), in_hbm(diagonal.reshape(tang * rloc, ax)),
     )

time: 61.5 us -> 61 us (level)
  local copies, waits for them, and re-layouts: 0.7 us -> 0 us
    unnamed x14 -> x0, local copies, waits for them, and re-layouts: 0.7 us -> none
where the time goes in v3:
time: 61 us; the launch traced here: 60.8 us
  Pallas kernels  59.5 us (98%)
  between operations  1.29 us (2%)
    pallas_call x1, Pallas kernels, body(): pl.pallas_call(functools.partial(kernel, dofs), out_shape=(jax.ShapeDtype...  58.6 us

profile of v3, /device:TPU:2, one launch (start us, length us, event | category | flops | bytes accessed | tf_op | source)
XLA Modules:
  0.0 60.8 jit_solution(959372067960802411)
XLA Ops:
  1.3 58.6 %sweeps.1 = (f32[4,3,64,128]{3,2,1,0:T(8,128)S(1)}, f32[4,3,64,128]{3,2,1,0:T(8,128)S(1)}) custom-call(s32[2,128]{1,0:T(2,128)} %bitcast.14, s32[2,128]{1,0:T(2,128)} %bitcast.15, s32[2,128]{1,0:T(2,128)} %bitcast.16, f32[2,128]{1,0:T(2,128)} %bitcast.17, f32[3,3]{1,0:T(4,128)} %kap.1, s32[1]{0:T(128)S(6)} %copy.14.cid, f32[8]{0:T(128)} %cst.1, f32[4]{0:T(128)} %shf.1, ...), custom_call_target="tpu_custom_call" | custom-call | tf_op jit(solution)/shard_map/sweeps/pallas_call | solution.py:622
  59.9 0.9 %store.1 = (f32[4,3,64,128]{3,2,1,0:T(8,128)}, f32[4,3,64,128]{3,2,1,0:T(8,128)}) custom-call(f32[4,3,64,128]{3,2,1,0:T(8,128)S(1)} %get-tuple-element.6.a, f32[4,3,64,128]{3,2,1,0:T(8,128)S(1)} %get-tuple-element.7.b), custom_call_target="tpu_custom_call" | custom-call | tf_op jit(solution)/shard_map/store/pallas_call | solution.py:637
